TPU v7x, 1024 devices: a whole 4x4x32 slice. The times are simulated.
1024 devices in a mesh: dom: 64 (over z, core), sub: 16 (over y, x).
Axes of the slice: x: 4, y: 4, z: 32, core: 2. Of those that a mesh axis runs over, the one named last changes fastest.
Arguments:
- coupling: bfloat16 [8192, 6, 128, 128], P(('dom', 'sub')), may hold values from -0.25 to 0.25
- diag_inv: bfloat16 [8192, 128, 128], P(('dom', 'sub')), may hold values from -0.5 to 0.5
- rhs: float32 [8192, 64, 128], P(('dom', 'sub')), may hold values from -6 to 6
- color: int32 [8192], P(('dom', 'sub')), may hold values from 0 to 3, as said below
- local_target: int32 [8192, 2], P(('dom', 'sub')), may hold values from 0 to 7, as said below
- group_peer: int32 [8192, 2], P(('dom', 'sub')), may hold values from 0 to 15, as said below
- group_list: int32 [1024, 4, 16], P(('dom', 'sub')), may hold values from -1 to 7, as said below
- dom_target: int32 [8192, 2], P(('dom', 'sub')), may hold values from 0 to 7, as said below
Outputs:
- solution: float32 [8192, 64, 128], P(('dom', 'sub'))
- defect: float32 [8192, 64, 128], P(('dom', 'sub'))
Inputs may be any that keep to these rules, and one draw needn't show every extreme that they name: Each partition window of 8 consecutive block rows holds exactly a quarter of its rows of each color. `local_target`: A row of another color than row i, in the same partition window. `group_peer`: never the row's own member of the group; the two entries of a row differ. `group_list`: entry [p, c, q] is the local index on member q of p's group of a row of another color than c that receives all of p's color-c couplings to q, and -1 where p has none; a partition sends at most one row's sum to each member in a color. `dom_target`: groups form a cycle; the row reached is always of another color than row i.
All inputs are finite; a program needn't handle non-finite values.
Results may differ from a plain program's by a relative error of at most 0.012.
Values sent between devices are 32-bit elements; how exact they have to be, the bound alone decides.
A program may use at most 32 MiB of HBM per device.

v0:
```python
import jax
import jax.numpy as jnp
from jax import lax
from jax.sharding import PartitionSpec as P

COLORS = 4
SWEEPS = 2
COUPLINGS = 6


def extended(value, sides, width):
    for axis, dim in sides:
        devices, length = (lax.axis_size(axis), value.shape[dim])
        up = [(i, (i + 1) % devices) for i in range(devices)]
        down = [(j, i) for i, j in up]
        last = lax.slice_in_dim(value, length - width, length, axis=dim)
        first = lax.slice_in_dim(value, 0, width, axis=dim)
        before = lax.ppermute(last, axis, up)
        after = lax.ppermute(first, axis, down)
        value = jnp.concatenate([before, value, after], axis=dim)
    return value


def on_device(coupling, diag_inv, rhs, color, local_target, group_peer, group_list, dom_target):
    rows_dev, rhs_count, block_width = rhs.shape
    quarter = rows_dev // COLORS
    group_size = lax.axis_size("sub")
    members = jnp.arange(group_size, dtype=jnp.int32)
    order_flat = jnp.argsort(color, stable=True)
    rank_of = jnp.argsort(order_flat)
    by_color = order_flat.reshape(COLORS, quarter)
    peer_by = group_peer[by_color]
    local_by = local_target[by_color]
    dom_by = dom_target[by_color]
    sorted_coupling = coupling[order_flat].reshape(
        COLORS, quarter, COUPLINGS, block_width, block_width
    )
    local_tiles = sorted_coupling[:, :, 0:2]
    group_tiles = sorted_coupling[:, :, 2:4]
    cycle_tiles = jnp.stack([sorted_coupling[:, :, 5], sorted_coupling[:, :, 4]], axis=1)
    diag_sorted = diag_inv[order_flat].reshape(COLORS, quarter, block_width, block_width)
    rhs_sorted = rhs[order_flat]
    dom_table = jnp.stack([dom_by[:, :, 1], dom_by[:, :, 0]])
    dom_lists = extended(dom_table, (("dom", 0),), 1)
    from_below = dom_lists[0]
    from_above = dom_lists[3]
    incoming = lax.all_to_all(group_list, "sub", split_axis=2, concat_axis=2, tiled=True)[0]
    solution = jnp.zeros(rhs.shape, jnp.float32).reshape(COLORS, quarter, rhs_count, block_width)
    coupled = jnp.zeros(rhs.shape, jnp.float32)
    for sweep_no in range(SWEEPS):
        for color_now in range(COLORS):
            start_row = color_now * quarter
            current = coupled[start_row : start_row + quarter]
            update_in = (rhs_sorted[start_row : start_row + quarter] - current).astype(jnp.bfloat16)
            updated = jnp.einsum(
                "prb,pbe->pre",
                update_in,
                diag_sorted[color_now],
                preferred_element_type=jnp.float32,
            )
            change = (updated - solution[color_now]).astype(jnp.bfloat16)
            solution = solution.at[color_now].set(updated)
            local_items = jnp.einsum(
                "prb,pkbe->pkre", change, local_tiles[color_now], preferred_element_type=jnp.float32
            ).reshape(2 * quarter, rhs_count * block_width)
            group_terms = jnp.einsum(
                "prb,pkbe->pkre", change, group_tiles[color_now], preferred_element_type=jnp.float32
            ).reshape(2 * quarter, rhs_count * block_width)
            dom_send = jnp.einsum(
                "prb,kpbe->kpre", change, cycle_tiles[color_now], preferred_element_type=jnp.float32
            )
            local_sel = local_by[color_now].reshape(-1)[None, :] == order_flat[:, None]
            peer_onehot = (peer_by[color_now].reshape(-1)[None, :] == members[:, None]).astype(
                jnp.float32
            )
            sendbuf = jnp.dot(peer_onehot, group_terms, precision=lax.Precision.HIGHEST).reshape(
                group_size, rhs_count, block_width
            )
            arrived = lax.all_to_all(sendbuf, "sub", split_axis=0, concat_axis=0, tiled=True)
            group_items = arrived.reshape(group_size, rhs_count * block_width)
            group_sel = incoming[color_now][None, :] == order_flat[:, None]
            dom_got = extended(dom_send, (("dom", 0),), 1)
            dom_items = jnp.concatenate([dom_got[0], dom_got[3]], axis=0).reshape(
                2 * quarter, rhs_count * block_width
            )
            dom_rows = jnp.concatenate([from_below[color_now], from_above[color_now]], axis=0)
            dom_sel = dom_rows[None, :] == order_flat[:, None]
            selector = jnp.concatenate([local_sel, group_sel, dom_sel], axis=1).astype(jnp.float32)
            arrived_items = jnp.concatenate([local_items, group_items, dom_items], axis=0)
            added = jnp.dot(selector, arrived_items, precision=lax.Precision.HIGHEST)
            coupled = coupled + added.reshape(rows_dev, rhs_count, block_width)
    solution_rows = solution.reshape(rows_dev, rhs_count, block_width)[rank_of]
    defect_rows = (rhs_sorted - coupled)[rank_of]
    return (solution_rows, defect_rows)


def solution(mesh):
    placed = (
        P(("dom", "sub"), None, None, None),
        P(("dom", "sub"), None, None),
        P(("dom", "sub"), None, None),
        P(("dom", "sub")),
        P(("dom", "sub"), None),
        P(("dom", "sub"), None),
        P(("dom", "sub"), None, None),
        P(("dom", "sub"), None),
    )
    return jax.shard_map(
        on_device,
        mesh=mesh,
        in_specs=placed,
        out_specs=(P(("dom", "sub"), None, None), P(("dom", "sub"), None, None)),
        check_vma=False,
    )
```

profile of v0, /device:TPU:6, one launch (start us, length us, event | category | flops | bytes accessed | tf_op | source)
XLA Modules:
  0.0 242.3 jit_solution(16789106331238996190)
XLA Ops:
  0.7 1.7 sort.34
  5.3 16.2 %collective-permute-start.1 = (s32[1,4,2]{1,2,0:T(2,128)}, s32[1,4,2]{1,2,0:T(2,128)}, u32[]{:S(2)}, u32[]{:S(2)}) collective-permute-start(s32[1,4,2]{1,2,0:T(2,128)} %bitcast.3), channel_id=1, source_target_pairs={{16,0},{32,16},{48,32},{64,48},{80,64},{96,80},{112,96},{128,112},... | collective-permute-start | bytes 104 | tf_op jit(solution)/shard_map/ppermute | solution.py:19
  26.2 2.2 gather_fusion.1
  28.5 1.8 fusion.80
  33.5 7.4 %all-to-all-start = ((s32[1,4,16]{1,0,2:T(1,128)}), s32[1,4,16]{1,0,2:T(1,128)S(1)}, u32[]{:S(2)}, u32[]{:S(2)}) async-start(s32[1,4,16]{1,0,2:T(1,128)} %copy.73), calls=%async_computation | async-start | bytes 16384 | tf_op jit(solution)/shard_map/all_to_all | solution.py:47
  64.3 7.2 %all-to-all-start.1 = ((f32[16,64,128]{2,1,0:T(8,128)}), f32[16,64,128]{2,1,0:T(8,128)}, u32[]{:S(2)}, u32[]{:S(2)}) async-start(f32[16,64,128]{2,1,0:T(8,128)} %copy.79), calls=%async_computation.1 | async-start | bytes 1048576 | tf_op jit(solution)/shard_map/all_to_all | solution.py:79
  76.5 3.5 %all-to-all-done.1 = f32[16,64,128]{2,1,0:T(8,128)} async-done(((f32[16,64,128]{2,1,0:T(8,128)}), f32[16,64,128]{2,1,0:T(8,128)}, u32[]{:S(2)}, u32[]{:S(2)}) %all-to-all-start.1) | async-done | bytes 524320 | tf_op jit(solution)/shard_map/all_to_all | solution.py:79
  82.8 1.7 bitcast_dynamic-update-slice_fusion.6
  86.6 6.7 %all-to-all-start.2 = ((f32[16,64,128]{2,1,0:T(8,128)}), f32[16,64,128]{2,1,0:T(8,128)}, u32[]{:S(2)}, u32[]{:S(2)}) async-start(f32[16,64,128]{2,1,0:T(8,128)} %copy.82), calls=%async_computation.2 | async-start | bytes 1048576 | tf_op jit(solution)/shard_map/all_to_all | solution.py:79
  94.3 2.1 collective-permute-start.5
  97.3 1.7 copy.300
  104.9 1.7 bitcast_dynamic-update-slice_fusion.5
  109.6 7.3 %all-to-all-start.3 = ((f32[16,64,128]{2,1,0:T(8,128)}), f32[16,64,128]{2,1,0:T(8,128)}, u32[]{:S(2)}, u32[]{:S(2)}) async-start(f32[16,64,128]{2,1,0:T(8,128)} %copy.84), calls=%async_computation.3 | async-start | bytes 1048576 | tf_op jit(solution)/shard_map/all_to_all | solution.py:79
  119.7 1.7 copy.301
  127.4 1.7 bitcast_dynamic-update-slice_fusion.4
  132.1 7.0 %all-to-all-start.4 = ((f32[16,64,128]{2,1,0:T(8,128)}), f32[16,64,128]{2,1,0:T(8,128)}, u32[]{:S(2)}, u32[]{:S(2)}) async-start(f32[16,64,128]{2,1,0:T(8,128)} %copy.86), calls=%async_computation.4 | async-start | bytes 1048576 | tf_op jit(solution)/shard_map/all_to_all | solution.py:79
  142.6 1.7 copy.302
  148.2 1.6 convolution_add_fusion.4
  149.9 1.7 bitcast_dynamic-update-slice_fusion.3
  154.6 6.8 %all-to-all-start.5 = ((f32[16,64,128]{2,1,0:T(8,128)}), f32[16,64,128]{2,1,0:T(8,128)}, u32[]{:S(2)}, u32[]{:S(2)}) async-start(f32[16,64,128]{2,1,0:T(8,128)} %copy.88), calls=%async_computation.5 | async-start | bytes 1048576 | tf_op jit(solution)/shard_map/all_to_all | solution.py:79
  165.7 1.7 copy.303
  172.6 1.7 bitcast_dynamic-update-slice_fusion.2
  177.3 7.2 %all-to-all-start.6 = ((f32[16,64,128]{2,1,0:T(8,128)}), f32[16,64,128]{2,1,0:T(8,128)}, u32[]{:S(2)}, u32[]{:S(2)}) async-start(f32[16,64,128]{2,1,0:T(8,128)} %copy.90), calls=%async_computation.6 | async-start | bytes 1048576 | tf_op jit(solution)/shard_map/all_to_all | solution.py:79
  188.8 1.7 copy.304
  194.1 1.6 convolution_add_fusion.2
  195.7 1.7 bitcast_dynamic-update-slice_fusion.1
  200.4 7.2 %all-to-all-start.7 = ((f32[16,64,128]{2,1,0:T(8,128)}), f32[16,64,128]{2,1,0:T(8,128)}, u32[]{:S(2)}, u32[]{:S(2)}) async-start(f32[16,64,128]{2,1,0:T(8,128)} %copy.92), calls=%async_computation.7 | async-start | bytes 1048576 | tf_op jit(solution)/shard_map/all_to_all | solution.py:79
  211.9 1.7 copy.305
  218.9 1.7 bitcast_dynamic-update-slice_fusion
  223.5 7.2 %all-to-all-start.8 = ((f32[16,64,128]{2,1,0:T(8,128)}), f32[16,64,128]{2,1,0:T(8,128)}, u32[]{:S(2)}, u32[]{:S(2)}) async-start(f32[16,64,128]{2,1,0:T(8,128)} %copy.94), calls=%async_computation.8 | async-start | bytes 1048576 | tf_op jit(solution)/shard_map/all_to_all | solution.py:79
  234.8 2.2 gather_fusion.6
  237.1 1.8 collective-permute-done.16
  (258 shorter events, 120.1 us)
Async XLA Ops:
  0.6 22.4 %copy-start = (bf16[8,6,128,128]{3,2,1,0:T(8,128)(2,1)S(1)}, bf16[8,6,128,128]{3,2,1,0:T(8,128)(2,1)}, u32[]{:S(2)}) copy-start(bf16[8,6,128,128]{3,2,1,0:T(8,128)(2,1)} %param.24) | copy-start | bytes 4718596
  2.4 21.5 %copy-start.21 = (s32[8]{0:T(128)}, s32[8]{0:T(128)S(1)}, u32[]{:S(2)}) copy-start(s32[8]{0:T(128)S(1)} %get-tuple-element.100) | copy-start | bytes 100
  4.6 57.4 %collective-permute-start = (s32[1,4,2]{1,2,0:T(2,128)}, s32[1,4,2]{1,2,0:T(2,128)}, u32[]{:S(2)}, u32[]{:S(2)}) collective-permute-start(s32[1,4,2]{1,2,0:T(2,128)} %bitcast.2), channel_id=1, source_target_pairs={{0,16},{16,32},{32,48},{48,64},{64,80},{80,96},{96,112},{112,128},... | collective-permute-start | bytes 104 | tf_op jit(solution)/shard_map/ppermute | solution.py:18
  5.3 57.8 %collective-permute-start.1 = (s32[1,4,2]{1,2,0:T(2,128)}, s32[1,4,2]{1,2,0:T(2,128)}, u32[]{:S(2)}, u32[]{:S(2)}) collective-permute-start(s32[1,4,2]{1,2,0:T(2,128)} %bitcast.3), channel_id=1, source_target_pairs={{16,0},{32,16},{48,32},{64,48},{80,64},{96,80},{112,96},{128,112},... | collective-permute-start | bytes 104 | tf_op jit(solution)/shard_map/ppermute | solution.py:19
  32.1 42.8 %collective-permute-start.3 = (f32[1,2,64,128]{3,2,0,1:T(8,128)}, f32[1,2,64,128]{3,2,0,1:T(8,128)}, u32[]{:S(2)}, u32[]{:S(2)}) collective-permute-start(f32[1,2,64,128]{3,2,0,1:T(8,128)} %get-tuple-element.135), channel_id=1, source_target_pairs={{16,0},{32,16},{48,32},{64,48},{80,64},{96,80},{112,96},{128,112},... | collective-permute-start | bytes 196616 | tf_op jit(solution)/shard_map/ppermute | solution.py:19
  32.8 43.0 %collective-permute-start.2 = (f32[1,2,64,128]{3,2,0,1:T(8,128)}, f32[1,2,64,128]{3,2,0,1:T(8,128)S(1)}, u32[]{:S(2)}, u32[]{:S(2)}) collective-permute-start(f32[1,2,64,128]{3,2,0,1:T(8,128)} %get-tuple-element.134), channel_id=1, source_target_pairs={{0,16},{16,32},{32,48},{48,64},{64,80},{80,96},{96,112},{112,128},... | collective-permute-start | bytes 196616 | tf_op jit(solution)/shard_map/ppermute | solution.py:18
  33.5 30.8 %all-to-all-start = ((s32[1,4,16]{1,0,2:T(1,128)}), s32[1,4,16]{1,0,2:T(1,128)S(1)}, u32[]{:S(2)}, u32[]{:S(2)}) async-start(s32[1,4,16]{1,0,2:T(1,128)} %copy.73), calls=%async_computation | async-start | bytes 16384 | tf_op jit(solution)/shard_map/all_to_all | solution.py:47
  53.7 17.8 %copy-start.22 = (s32[8]{0:T(128)S(1)}, s32[8]{0:T(128)}, u32[]{:S(2)}) copy-start(s32[8]{0:T(128)} %copy-done.21) | copy-start | bytes 100
  64.3 15.7 %all-to-all-start.1 = ((f32[16,64,128]{2,1,0:T(8,128)}), f32[16,64,128]{2,1,0:T(8,128)}, u32[]{:S(2)}, u32[]{:S(2)}) async-start(f32[16,64,128]{2,1,0:T(8,128)} %copy.79), calls=%async_computation.1 | async-start | bytes 1048576 | tf_op jit(solution)/shard_map/all_to_all | solution.py:79
  86.6 15.3 %all-to-all-start.2 = ((f32[16,64,128]{2,1,0:T(8,128)}), f32[16,64,128]{2,1,0:T(8,128)}, u32[]{:S(2)}, u32[]{:S(2)}) async-start(f32[16,64,128]{2,1,0:T(8,128)} %copy.82), calls=%async_computation.2 | async-start | bytes 1048576 | tf_op jit(solution)/shard_map/all_to_all | solution.py:79
  94.3 4.8 %collective-permute-start.5 = (f32[1,2,64,128]{3,2,0,1:T(8,128)S(1)}, f32[1,2,64,128]{3,2,0,1:T(8,128)S(1)}, u32[]{:S(2)}, u32[]{:S(2)}) collective-permute-start(f32[1,2,64,128]{3,2,0,1:T(8,128)S(1)} %get-tuple-element.133), channel_id=1, source_target_pairs={{16,0},{32,16},{48,32},{64,48},{80,64},{96,80},{112,96},{128,112},... | collective-permute-start | bytes 196616 | tf_op jit(solution)/shard_map/ppermute | solution.py:19
  96.3 4.9 %collective-permute-start.4 = (f32[1,2,64,128]{3,2,0,1:T(8,128)S(1)}, f32[1,2,64,128]{3,2,0,1:T(8,128)S(1)}, u32[]{:S(2)}, u32[]{:S(2)}) collective-permute-start(f32[1,2,64,128]{3,2,0,1:T(8,128)S(1)} %get-tuple-element.132), channel_id=1, source_target_pairs={{0,16},{16,32},{32,48},{48,64},{64,80},{80,96},{96,112},{112,128},... | collective-permute-start | bytes 196616 | tf_op jit(solution)/shard_map/ppermute | solution.py:18
  106.6 10.3 %copy-start.2 = (bf16[2,2,128,128]{3,2,1,0:T(8,128)(2,1)S(1)}, bf16[2,2,128,128]{3,2,1,0:T(8,128)(2,1)}, u32[]{:S(2)}) copy-start(bf16[2,2,128,128]{3,2,1,0:T(8,128)(2,1)} %get-tuple-element.119) | copy-start | bytes 393220
  109.6 14.9 %all-to-all-start.3 = ((f32[16,64,128]{2,1,0:T(8,128)}), f32[16,64,128]{2,1,0:T(8,128)}, u32[]{:S(2)}, u32[]{:S(2)}) async-start(f32[16,64,128]{2,1,0:T(8,128)} %copy.84), calls=%async_computation.3 | async-start | bytes 1048576 | tf_op jit(solution)/shard_map/all_to_all | solution.py:79
  117.8 3.6 %collective-permute-start.7 = (f32[1,2,64,128]{3,2,0,1:T(8,128)S(1)}, f32[1,2,64,128]{3,2,0,1:T(8,128)S(1)}, u32[]{:S(2)}, u32[]{:S(2)}) collective-permute-start(f32[1,2,64,128]{3,2,0,1:T(8,128)S(1)} %get-tuple-element.131), channel_id=1, source_target_pairs={{16,0},{32,16},{48,32},{64,48},{80,64},{96,80},{112,96},{128,112},... | collective-permute-start | bytes 196616 | tf_op jit(solution)/shard_map/ppermute | solution.py:19
  118.7 4.9 %collective-permute-start.6 = (f32[1,2,64,128]{3,2,0,1:T(8,128)S(1)}, f32[1,2,64,128]{3,2,0,1:T(8,128)S(1)}, u32[]{:S(2)}, u32[]{:S(2)}) collective-permute-start(f32[1,2,64,128]{3,2,0,1:T(8,128)S(1)} %get-tuple-element.130), channel_id=1, source_target_pairs={{0,16},{16,32},{32,48},{48,64},{64,80},{80,96},{96,112},{112,128},... | collective-permute-start | bytes 196616 | tf_op jit(solution)/shard_map/ppermute | solution.py:18
  129.1 10.0 %copy-start.1 = (bf16[2,2,128,128]{3,2,1,0:T(8,128)(2,1)S(1)}, bf16[2,2,128,128]{3,2,1,0:T(8,128)(2,1)}, u32[]{:S(2)}) copy-start(bf16[2,2,128,128]{3,2,1,0:T(8,128)(2,1)} %get-tuple-element.116) | copy-start | bytes 393220
  132.1 14.8 %all-to-all-start.4 = ((f32[16,64,128]{2,1,0:T(8,128)}), f32[16,64,128]{2,1,0:T(8,128)}, u32[]{:S(2)}, u32[]{:S(2)}) async-start(f32[16,64,128]{2,1,0:T(8,128)} %copy.86), calls=%async_computation.4 | async-start | bytes 1048576 | tf_op jit(solution)/shard_map/all_to_all | solution.py:79
  140.1 4.2 %collective-permute-start.9 = (f32[1,2,64,128]{3,2,0,1:T(8,128)S(1)}, f32[1,2,64,128]{3,2,0,1:T(8,128)S(1)}, u32[]{:S(2)}, u32[]{:S(2)}) collective-permute-start(f32[1,2,64,128]{3,2,0,1:T(8,128)S(1)} %get-tuple-element.129), channel_id=1, source_target_pairs={{16,0},{32,16},{48,32},{64,48},{80,64},{96,80},{112,96},{128,112},... | collective-permute-start | bytes 196616 | tf_op jit(solution)/shard_map/ppermute | solution.py:19
  140.9 4.9 %collective-permute-start.8 = (f32[1,2,64,128]{3,2,0,1:T(8,128)S(1)}, f32[1,2,64,128]{3,2,0,1:T(8,128)S(1)}, u32[]{:S(2)}, u32[]{:S(2)}) collective-permute-start(f32[1,2,64,128]{3,2,0,1:T(8,128)S(1)} %get-tuple-element.128), channel_id=1, source_target_pairs={{0,16},{16,32},{32,48},{48,64},{64,80},{80,96},{96,112},{112,128},... | collective-permute-start | bytes 196616 | tf_op jit(solution)/shard_map/ppermute | solution.py:18
  154.6 15.0 %all-to-all-start.5 = ((f32[16,64,128]{2,1,0:T(8,128)}), f32[16,64,128]{2,1,0:T(8,128)}, u32[]{:S(2)}, u32[]{:S(2)}) async-start(f32[16,64,128]{2,1,0:T(8,128)} %copy.88), calls=%async_computation.5 | async-start | bytes 1048576 | tf_op jit(solution)/shard_map/all_to_all | solution.py:79
  162.5 4.9 %collective-permute-start.11 = (f32[1,2,64,128]{3,2,0,1:T(8,128)S(1)}, f32[1,2,64,128]{3,2,0,1:T(8,128)S(1)}, u32[]{:S(2)}, u32[]{:S(2)}) collective-permute-start(f32[1,2,64,128]{3,2,0,1:T(8,128)S(1)} %get-tuple-element.127), channel_id=1, source_target_pairs={{16,0},{32,16},{48,32},{64,48},{80,64},{96,80},{112,96},{128,112},... | collective-permute-start | bytes 196616 | tf_op jit(solution)/shard_map/ppermute | solution.py:19
  164.0 4.9 %collective-permute-start.10 = (f32[1,2,64,128]{3,2,0,1:T(8,128)S(1)}, f32[1,2,64,128]{3,2,0,1:T(8,128)S(1)}, u32[]{:S(2)}, u32[]{:S(2)}) collective-permute-start(f32[1,2,64,128]{3,2,0,1:T(8,128)S(1)} %get-tuple-element.126), channel_id=1, source_target_pairs={{0,16},{16,32},{32,48},{48,64},{64,80},{80,96},{96,112},{112,128},... | collective-permute-start | bytes 196616 | tf_op jit(solution)/shard_map/ppermute | solution.py:18
  177.3 15.4 %all-to-all-start.6 = ((f32[16,64,128]{2,1,0:T(8,128)}), f32[16,64,128]{2,1,0:T(8,128)}, u32[]{:S(2)}, u32[]{:S(2)}) async-start(f32[16,64,128]{2,1,0:T(8,128)} %copy.90), calls=%async_computation.6 | async-start | bytes 1048576 | tf_op jit(solution)/shard_map/all_to_all | solution.py:79
  185.6 4.9 %collective-permute-start.13 = (f32[1,2,64,128]{3,2,0,1:T(8,128)S(1)}, f32[1,2,64,128]{3,2,0,1:T(8,128)S(1)}, u32[]{:S(2)}, u32[]{:S(2)}) collective-permute-start(f32[1,2,64,128]{3,2,0,1:T(8,128)S(1)} %get-tuple-element.125), channel_id=1, source_target_pairs={{16,0},{32,16},{48,32},{64,48},{80,64},{96,80},{112,96},{128,112},... | collective-permute-start | bytes 196616 | tf_op jit(solution)/shard_map/ppermute | solution.py:19
  187.1 4.9 %collective-permute-start.12 = (f32[1,2,64,128]{3,2,0,1:T(8,128)S(1)}, f32[1,2,64,128]{3,2,0,1:T(8,128)S(1)}, u32[]{:S(2)}, u32[]{:S(2)}) collective-permute-start(f32[1,2,64,128]{3,2,0,1:T(8,128)S(1)} %get-tuple-element.124), channel_id=1, source_target_pairs={{0,16},{16,32},{32,48},{48,64},{64,80},{80,96},{96,112},{112,128},... | collective-permute-start | bytes 196616 | tf_op jit(solution)/shard_map/ppermute | solution.py:18
  200.4 15.5 %all-to-all-start.7 = ((f32[16,64,128]{2,1,0:T(8,128)}), f32[16,64,128]{2,1,0:T(8,128)}, u32[]{:S(2)}, u32[]{:S(2)}) async-start(f32[16,64,128]{2,1,0:T(8,128)} %copy.92), calls=%async_computation.7 | async-start | bytes 1048576 | tf_op jit(solution)/shard_map/all_to_all | solution.py:79
  208.7 4.9 %collective-permute-start.15 = (f32[1,2,64,128]{3,2,0,1:T(8,128)S(1)}, f32[1,2,64,128]{3,2,0,1:T(8,128)S(1)}, u32[]{:S(2)}, u32[]{:S(2)}) collective-permute-start(f32[1,2,64,128]{3,2,0,1:T(8,128)S(1)} %get-tuple-element.123), channel_id=1, source_target_pairs={{16,0},{32,16},{48,32},{64,48},{80,64},{96,80},{112,96},{128,112},... | collective-permute-start | bytes 196616 | tf_op jit(solution)/shard_map/ppermute | solution.py:19
  210.3 4.9 %collective-permute-start.14 = (f32[1,2,64,128]{3,2,0,1:T(8,128)S(1)}, f32[1,2,64,128]{3,2,0,1:T(8,128)S(1)}, u32[]{:S(2)}, u32[]{:S(2)}) collective-permute-start(f32[1,2,64,128]{3,2,0,1:T(8,128)S(1)} %get-tuple-element.122), channel_id=1, source_target_pairs={{0,16},{16,32},{32,48},{48,64},{64,80},{80,96},{96,112},{112,128},... | collective-permute-start | bytes 196616 | tf_op jit(solution)/shard_map/ppermute | solution.py:18
  223.5 15.5 %all-to-all-start.8 = ((f32[16,64,128]{2,1,0:T(8,128)}), f32[16,64,128]{2,1,0:T(8,128)}, u32[]{:S(2)}, u32[]{:S(2)}) async-start(f32[16,64,128]{2,1,0:T(8,128)} %copy.94), calls=%async_computation.8 | async-start | bytes 1048576 | tf_op jit(solution)/shard_map/all_to_all | solution.py:79
  232.3 4.7 %collective-permute-start.17 = (f32[1,2,64,128]{3,2,0,1:T(8,128)}, f32[1,2,64,128]{3,2,0,1:T(8,128)S(1)}, u32[]{:S(2)}, u32[]{:S(2)}) collective-permute-start(f32[1,2,64,128]{3,2,0,1:T(8,128)} %get-tuple-element.121), channel_id=1, source_target_pairs={{16,0},{32,16},{48,32},{64,48},{80,64},{96,80},{112,96},{128,112},... | collective-permute-start | bytes 196616 | tf_op jit(solution)/shard_map/ppermute | solution.py:19
  233.8 5.1 %collective-permute-start.16 = (f32[1,2,64,128]{3,2,0,1:T(8,128)}, f32[1,2,64,128]{3,2,0,1:T(8,128)S(1)}, u32[]{:S(2)}, u32[]{:S(2)}) collective-permute-start(f32[1,2,64,128]{3,2,0,1:T(8,128)} %get-tuple-element.120), channel_id=1, source_target_pairs={{0,16},{16,32},{32,48},{48,64},{64,80},{80,96},{96,112},{112,128},... | collective-permute-start | bytes 196616 | tf_op jit(solution)/shard_map/ppermute | solution.py:18
  (32 other events, 165.2 us)
where the time goes:
time: 247 us; the launch traced here: 242 us
  starting transfers between devices  90.9 us (37%)
  local copies, waits for them, and re-layouts  79 us (32%)
  matrix products  45.3 us (18%)
  other arithmetic  13.1 us (5%)
  waiting for transfers between devices  12.6 us (5%)
    all_to_all x8, starting transfers between devices, on_device(): lax.all_to_all(sendbuf, 'sub', split_axis=0, concat_axis=0, tiled=True)  56.7 us
    unnamed x123, local copies, waits for them, and re-layouts  41.1 us
    ppermute x9, starting transfers between devices, extended(): after = lax.ppermute(first, axis, down)  26.8 us
    dot_general x8, matrix products, on_device(): jnp.einsum('prb,pbe->pre', update_in, diag_sorted[color_now], preferred_e...  12.7 us
    dot_general x8, matrix products, on_device(): added = jnp.dot(selector, arrived_items, precision=lax.Precision.HIGHEST)  11.5 us
    ppermute x9, waiting for transfers between devices, extended(): before = lax.ppermute(last, axis, up)  8.43 us
    dot_general x8, local copies, waits for them, and re-layouts, on_device(): jnp.dot(peer_onehot, group_terms, precision=lax.Precision.HIGHEST)  7.84 us
    all_to_all x1, starting transfers between devices, on_device(): lax.all_to_all(group_list, 'sub', split_axis=2, concat_axis=2, tiled=True)  7.42 us
  transfers between devices with their start and end apart: 27, of which 10 were waited for; matrix products, arithmetic and copies ran while one was open for 32% of the time, Pallas kernels for 0%

commit v1 on v0

v1 whole, which is shorter than its diff:
```python
import functools

import jax
import jax.numpy as jnp
from jax import lax
from jax.experimental import pallas as pl
from jax.experimental.pallas import tpu as pltpu
from jax.sharding import PartitionSpec as P

MESH = pl.DeviceIdType.MESH
COLORS = 4
SWEEPS = 2
STEPS = COLORS * SWEEPS
SIDE = 4
OFFSETS = sorted(
    [(dx, dy) for dy in range(SIDE) for dx in range(SIDE) if (dx, dy) != (0, 0)],
    key=lambda o: -(min(o[0], SIDE - o[0]) + min(o[1], SIDE - o[1])),
)
PEERS = len(OFFSETS)
STREAMS = 2


def kernel(
    parts, group, coup, diag, rhs, color, ltgt, gpeer, glist, dtgt, sol_out, def_out,
    recv, drecv, send, dsend, tag_send, tag_recv, resid, solb, near, jrow, rank,
    rsem, ssem, tag_rsem, tag_ssem,
):
    me = lax.axis_index("sub")
    dom = lax.axis_index("dom")
    me_x, me_y = me % SIDE, me // SIDE
    peers = [((me_y + dy) % SIDE) * SIDE + (me_x + dx) % SIDE for dx, dy in OFFSETS]
    above, below = (dom + 1) % group, (dom + group - 1) % group
    devices = [{"sub": q} for q in peers] + [{"dom": above}, {"dom": below}]
    rows_dev, rhs_count, width = rhs.shape
    rows = rhs_count // parts

    barrier = pltpu.get_barrier_semaphore()
    for d in devices:
        pl.semaphore_signal(barrier, inc=1, device_id=d, device_id_type=MESH)

    colors = [color[r] for r in range(rows_dev)]
    slots = []
    for c in range(COLORS):
        first, total = jnp.int32(rows_dev - 1), jnp.int32(0)
        for r in reversed(range(rows_dev)):
            hit = colors[r] == c
            first = jnp.where(hit, r, first)
            total = total + jnp.where(hit, r, 0)
        slots += [first, jnp.clip(total - first, 0, rows_dev - 1)]
    for s, j in enumerate(slots):
        jrow[s] = j
    for r in range(rows_dev):
        place = jnp.int32(0)
        for s, j in enumerate(slots):
            place = jnp.where(j == r, s, place)
        rank[r] = place
    for s, j in enumerate(slots):
        resid[s] = rhs[j]
    solb[...] = jnp.zeros_like(solb)

    line = lax.broadcasted_iota(jnp.int32, (8, width), 0)
    for n, q in enumerate(peers):
        tile = jnp.full((8, width), -1, jnp.int32)
        for c in range(COLORS):
            tile = jnp.where(line == c, glist[0, c, q], tile)
        tag_send[n] = tile
    for way in range(2):
        tile = jnp.full((8, width), -1, jnp.int32)
        for s, j in enumerate(slots):
            tile = jnp.where(line == s, dtgt[j, way], tile)
        tag_send[PEERS + way] = tile

    def tag_copy(n):
        return pltpu.make_async_remote_copy(
            src_ref=tag_send.at[n], dst_ref=tag_recv.at[n], send_sem=tag_ssem.at[n],
            recv_sem=tag_rsem.at[n], device_id=devices[n], device_id_type=MESH,
        )

    def copy(t, n, part):
        if n < PEERS:
            src, dst = send.at[t % 2, n, part], recv.at[t, n, part]
        else:
            src, dst = dsend.at[t % 2, n - PEERS, part], drecv.at[t, n - PEERS, part]
        return pltpu.make_async_remote_copy(
            src_ref=src, dst_ref=dst, send_sem=ssem.at[t % 2, n, part],
            recv_sem=rsem.at[t % 2, n, part], device_id=devices[n], device_id_type=MESH,
        )

    def gather(t, part, into):
        c = t % COLORS
        span = pl.ds(part * rows, rows)
        targets = [jrow[s] for s in into]
        totals = [resid[s, span, :] for s in into]
        for n in range(PEERS):
            tag = jnp.broadcast_to(tag_recv[n, pl.ds(c, 1), :], (rows, width))
            item = recv[t, n, part]
            totals = [x - jnp.where(tag == j, item, 0.0) for x, j in zip(totals, targets)]
        for way in range(2):
            for i in range(2):
                tag = jnp.broadcast_to(tag_recv[PEERS + way, pl.ds(2 * c + i, 1), :], (rows, width))
                item = drecv[t, way, part, i]
                totals = [x - jnp.where(tag == j, item, 0.0) for x, j in zip(totals, targets)]
        for s, x in zip(into, totals):
            resid[s, span, :] = x

    def pair(c):
        return [2 * (c % COLORS), 2 * (c % COLORS) + 1]

    def solve(t, part, first):
        c = t % COLORS
        span = pl.ds(part * rows, rows)
        if not first:
            for n in range(PEERS + 2):
                copy(t - 1, n, part).wait_recv()
            gather(t - 1, part, pair(c))
        changes = []
        for s in pair(c):
            new = jnp.dot(
                resid[s, span, :].astype(jnp.bfloat16), diag[jrow[s]], preferred_element_type=jnp.float32
            )
            changes.append((new - solb[s, span, :]).astype(jnp.bfloat16))
            solb[s, span, :] = new
        owners = [jrow[s] for s in pair(c)]

        def products(i, k):
            both = jnp.concatenate([coup[owners[i], k], coup[owners[i], k + 1]], axis=1)
            out = jnp.dot(changes[i], both, preferred_element_type=jnp.float32)
            return out[:, :width], out[:, width:]

        terms = [products(i, 2) for i in range(2)]
        wants = [[jnp.full((rows, width), gpeer[j, k], jnp.int32) for k in range(2)] for j in owners]
        for n, q in enumerate(peers):
            sums = [
                jnp.where(want[0] == q, term[0], jnp.where(want[1] == q, term[1], 0.0))
                for want, term in zip(wants, terms)
            ]
            send[t % 2, n, part] = sums[0] + sums[1]
        for i in range(2):
            up, down = products(i, 4)
            dsend[t % 2, 0, part, i] = up
            dsend[t % 2, 1, part, i] = down
        for i in range(2):
            near[part, i, 0], near[part, i, 1] = products(i, 0)

    def launch(t, part):
        for n in range(PEERS + 2):
            copy(t, n, part).start()

    def local(t, part):
        c = t % COLORS
        span = pl.ds(part * rows, rows)
        into = pair(c + 1) + pair(c + 2) + pair(c + 3)
        targets = [jrow[s] for s in into]
        totals = [resid[s, span, :] for s in into]
        for i, s in enumerate(pair(c)):
            for k in range(2):
                tag = jnp.full((rows, width), ltgt[jrow[s], k], jnp.int32)
                item = near[part, i, k]
                totals = [x - jnp.where(tag == j, item, 0.0) for x, j in zip(totals, targets)]
        for s, x in zip(into, totals):
            resid[s, span, :] = x

    for part in range(parts):
        solve(0, part, True)
    pl.semaphore_wait(barrier, PEERS + 2)
    for n in range(PEERS + 2):
        tag_copy(n).start()
    for part in range(parts):
        launch(0, part)
    for part in range(parts):
        local(0, part)
    for n in range(PEERS + 2):
        tag_copy(n).wait_recv()

    def step(t, carry):
        for part in range(parts):
            @pl.when(t >= 2)
            def _():
                for n in range(PEERS + 2):
                    copy(t, n, part).wait_send()

            solve(t, part, False)
            launch(t, part)
            local(t, part)
            gather(t - 1, part, pair(t + 1) + pair(t + 2))
        return carry

    lax.fori_loop(1, STEPS, step, 0)
    for r in range(rows_dev):
        sol_out[r] = solb[rank[r]]
    last = STEPS - 1
    for part in range(parts):
        for n in range(PEERS + 2):
            copy(last, n, part).wait_recv()
        gather(last, part, pair(0) + pair(1) + pair(2))
    for r in range(rows_dev):
        def_out[r] = resid[rank[r]]
    for part in range(parts):
        for n in range(PEERS + 2):
            copy(last - 1, n, part).wait_send()
            copy(last, n, part).wait_send()
    for n in range(PEERS + 2):
        tag_copy(n).wait_send()


def on_device(coupling, diag_inv, rhs, color, local_target, group_peer, group_list, dom_target):
    rows_dev, rhs_count, width = rhs.shape
    parts, rows = STREAMS, rhs_count // STREAMS
    vmem, smem = pl.BlockSpec(memory_space=pltpu.VMEM), pl.BlockSpec(memory_space=pltpu.SMEM)
    ends = PEERS + 2
    out = jax.ShapeDtypeStruct(rhs.shape, jnp.float32)
    return pl.pallas_call(
        functools.partial(kernel, parts, lax.axis_size("dom")),
        out_shape=(out, out),
        in_specs=[vmem] * 3 + [smem] * 5,
        out_specs=(vmem, vmem),
        scratch_shapes=[
            pltpu.VMEM((STEPS, PEERS, parts, rows, width), jnp.float32),
            pltpu.VMEM((STEPS, 2, parts, 2, rows, width), jnp.float32),
            pltpu.VMEM((2, PEERS, parts, rows, width), jnp.float32),
            pltpu.VMEM((2, 2, parts, 2, rows, width), jnp.float32),
            pltpu.VMEM((ends, 8, width), jnp.int32),
            pltpu.VMEM((ends, 8, width), jnp.int32),
            pltpu.VMEM((rows_dev, rhs_count, width), jnp.float32),
            pltpu.VMEM((rows_dev, rhs_count, width), jnp.float32),
            pltpu.VMEM((parts, 2, 2, rows, width), jnp.float32),
            pltpu.SMEM((rows_dev,), jnp.int32),
            pltpu.SMEM((rows_dev,), jnp.int32),
            pltpu.SemaphoreType.DMA((2, ends, parts)),
            pltpu.SemaphoreType.DMA((2, ends, parts)),
            pltpu.SemaphoreType.DMA((ends,)),
            pltpu.SemaphoreType.DMA((ends,)),
        ],
        compiler_params=pltpu.CompilerParams(collective_id=0, has_side_effects=True),
        name="sweeps",
    )(coupling, diag_inv, rhs, color, local_target, group_peer, group_list, dom_target)


def solution(mesh):
    placed = (
        P(("dom", "sub"), None, None, None),
        P(("dom", "sub"), None, None),
        P(("dom", "sub"), None, None),
        P(("dom", "sub")),
        P(("dom", "sub"), None),
        P(("dom", "sub"), None),
        P(("dom", "sub"), None, None),
        P(("dom", "sub"), None),
    )
    return jax.shard_map(
        on_device,
        mesh=mesh,
        in_specs=placed,
        out_specs=(P(("dom", "sub"), None, None), P(("dom", "sub"), None, None)),
        check_vma=False,
    )
```

time: 247 us -> 82.2 us (0.33); the launches traced: 242 us -> 81.6 us
  starting transfers between devices: 90.9 us -> 0 us
  Pallas kernels: 0 us -> 73.6 us
  local copies, waits for them, and re-layouts: 79 us -> 7.37 us
  matrix products: 45.3 us -> 0 us
  other arithmetic: 13.1 us -> 0 us
  waiting for transfers between devices: 12.6 us -> 0 us
    pallas_call x0 -> x1, Pallas kernels: none -> 73.6 us  [on_device(): pl.pallas_call(functools.partial(kernel, parts, lax.axis_size('dom')), ou...]
    all_to_all x9 -> x0, starting transfers between devices: 64.1 us -> none  [the longest x8 56.7 us: on_device(): lax.all_to_all(sendbuf, 'sub', split_axis=0, concat_axis=0, tiled=True)]
    dot_general x48 -> x0, matrix products: 45.3 us -> none  [the longest x8 12.7 us: on_device(): jnp.einsum('prb,pbe->pre', update_in, diag_sorted[color_now], preferred_e...]
    unnamed x123 -> x5, local copies, waits for them, and re-layouts: 41.1 us -> 7.37 us
    ppermute x18 -> x0, starting transfers between devices: 26.8 us -> none  [the longest x9 26.8 us: extended(): after = lax.ppermute(first, axis, down)]
    gather x8 -> x0, local copies, waits for them, and re-layouts: 10.9 us -> none  [the longest x1 2.23 us: on_device(): diag_inv[order_flat].reshape(COLORS, quarter, block_width, block_width)]
    slice x16 -> x0, local copies, waits for them, and re-layouts: 9.01 us -> none  [the longest x3 1.41 us: on_device(): dom_table = jnp.stack([dom_by[:, :, 1], dom_by[:, :, 0]])]
    ppermute x18 -> x0, waiting for transfers between devices: 8.45 us -> none  [the longest x9 8.43 us: extended(): before = lax.ppermute(last, axis, up)]
  transfers between devices with their start and end apart: 27 -> 0, of which waited for: 10 -> 0; matrix products, arithmetic and copies ran while one was open for 32% -> 0% of each run, Pallas kernels for 0% -> 0%
where the time goes in v1:
time: 82.2 us; the launch traced here: 81.6 us
  Pallas kernels  73.6 us (90%)
  local copies, waits for them, and re-layouts  7.37 us (9%)
    pallas_call x1, Pallas kernels, on_device(): pl.pallas_call(functools.partial(kernel, parts, lax.axis_size('dom')), ou...  73.6 us
    unnamed x5, local copies, waits for them, and re-layouts  7.37 us

profile of v1, /device:TPU:6, one launch (start us, length us, event | category | flops | bytes accessed | tf_op | source)
XLA Modules:
  0.0 81.6 jit_solution(9873855003002997614)
XLA Ops:
  0.6 1.3 %copy.10.ltgt = s32[8,2]{1,0:T(8,128)} copy(s32[8,2]{0,1:T(2,128)} %param.12) | data formatting | bytes 128 | tf_op args[4]
  2.0 1.3 %copy.11.gpeer = s32[8,2]{1,0:T(8,128)} copy(s32[8,2]{0,1:T(2,128)} %param.13) | data formatting | bytes 128 | tf_op args[5]
  3.3 1.3 %copy.12.dtgt = s32[8,2]{1,0:T(8,128)} copy(s32[8,2]{0,1:T(2,128)} %param.15) | data formatting | bytes 128 | tf_op args[7]
  4.7 73.6 %sweeps.1 = (f32[8,64,128]{2,1,0:T(8,128)}, f32[8,64,128]{2,1,0:T(8,128)}) custom-call(bf16[8,6,128,128]{3,2,1,0:T(8,128)(2,1)} %coup.1, bf16[8,128,128]{2,1,0:T(8,128)(2,1)} %diag.1, f32[8,64,128]{2,1,0:T(8,128)} %rhs.1, s32[8]{0:T(128)} %color.1, s32[8,2]{1,0:T(8,128)} %copy.10.ltgt, s32[8,2]{1,0:T(8,128)} %copy.11.gpeer, s32[1,4,16]{2,1,0:T(4,128)} %glist.1, ...), custom_call_target="tpu_custom_call" | custom-call | tf_op jit(solution)/shard_map/sweeps/pallas_call | solution.py:212
  78.3 1.7 %copy.15 = f32[8,64,128]{2,1,0:T(8,128)} copy(f32[8,64,128]{2,1,0:T(8,128)} %get-tuple-element.4) | data formatting | bytes 524288
  80.0 1.7 %copy.16 = f32[8,64,128]{2,1,0:T(8,128)} copy(f32[8,64,128]{2,1,0:T(8,128)} %get-tuple-element.5) | data formatting | bytes 524288

commit v2 on v1

v2 whole, which is shorter than its diff:
```python
import functools

import jax
import jax.numpy as jnp
from jax import lax
from jax.experimental import pallas as pl
from jax.experimental.pallas import tpu as pltpu
from jax.sharding import PartitionSpec as P

MESH = pl.DeviceIdType.MESH
COLORS = 4
SWEEPS = 2
STEPS = COLORS * SWEEPS
SIDE = 4
OFFSETS = sorted(
    [(dx, dy) for dy in range(SIDE) for dx in range(SIDE) if (dx, dy) != (0, 0)],
    key=lambda o: -(min(o[0], SIDE - o[0]) + min(o[1], SIDE - o[1])),
)
PEERS = len(OFFSETS)
ENDS = PEERS + 2
ITEMS = PEERS + 4
STREAMS = 4


def kernel(
    parts, group, coup_in, diag_in, rhs_in, color_in, ltgt_in, gpeer_in, glist_in, dtgt_in, sol_out, def_out,
    coup, diag, rhs, color, ltgt, gpeer, glist, dtgt,
    recv, send, tag_send, tag_recv, resid, solb, near, jrow, rank,
    in_sem, rsem, ssem, tag_rsem, tag_ssem,
):
    me = lax.axis_index("sub")
    dom = lax.axis_index("dom")
    me_x, me_y = me % SIDE, me // SIDE
    peers = [((me_y + dy) % SIDE) * SIDE + (me_x + dx) % SIDE for dx, dy in OFFSETS]
    above, below = (dom + 1) % group, (dom + group - 1) % group
    devices = [{"sub": q} for q in peers] + [{"dom": above}, {"dom": below}]
    rows_dev, rhs_count, width = rhs.shape
    rows = rhs_count // parts

    barrier = pltpu.get_barrier_semaphore()
    for d in devices:
        pl.semaphore_signal(barrier, inc=1, device_id=d, device_id_type=MESH)
    pairs = [
        (color_in, color), (dtgt_in, dtgt), (glist_in, glist), (rhs_in, rhs), (diag_in, diag),
        (gpeer_in, gpeer), (ltgt_in, ltgt), (coup_in, coup),
    ]
    loads = [pltpu.make_async_copy(src, dst, in_sem.at[n]) for n, (src, dst) in enumerate(pairs)]
    for load in loads:
        load.start()
    solb[...] = jnp.zeros_like(solb)

    loads[0].wait()
    colors = [color[r] for r in range(rows_dev)]
    slots = []
    for c in range(COLORS):
        first, total = jnp.int32(rows_dev - 1), jnp.int32(0)
        for r in reversed(range(rows_dev)):
            hit = colors[r] == c
            first = jnp.where(hit, r, first)
            total = total + jnp.where(hit, r, 0)
        slots += [first, jnp.clip(total - first, 0, rows_dev - 1)]
    for s, j in enumerate(slots):
        jrow[s] = j
    for r in range(rows_dev):
        place = jnp.int32(0)
        for s, j in enumerate(slots):
            place = jnp.where(j == r, s, place)
        rank[r] = place

    def tag_copy(n):
        return pltpu.make_async_remote_copy(
            src_ref=tag_send.at[n], dst_ref=tag_recv.at[n], send_sem=tag_ssem,
            recv_sem=tag_rsem, device_id=devices[n], device_id_type=MESH,
        )

    def all_tags():
        return pltpu.make_async_remote_copy(
            src_ref=tag_send, dst_ref=tag_recv, send_sem=tag_ssem,
            recv_sem=tag_rsem, device_id=devices[0], device_id_type=MESH,
        )

    def copy(t, part, n):
        at = n if n < PEERS else pl.ds(PEERS + 2 * (n - PEERS), 2)
        return pltpu.make_async_remote_copy(
            src_ref=send.at[t % 2, part, at], dst_ref=recv.at[t, part, at], send_sem=ssem.at[t % 2, part],
            recv_sem=rsem.at[t % 2, part], device_id=devices[n], device_id_type=MESH,
        )

    def all_copies(t, part):
        return pltpu.make_async_remote_copy(
            src_ref=send.at[t % 2, part], dst_ref=recv.at[t, part], send_sem=ssem.at[t % 2, part],
            recv_sem=rsem.at[t % 2, part], device_id=devices[0], device_id_type=MESH,
        )

    def pair(c):
        return [2 * (c % COLORS), 2 * (c % COLORS) + 1]

    def gather(t, part, into):
        c = t % COLORS
        span = pl.ds(part * rows, rows)
        targets = [jrow[s] for s in into]
        totals = [resid[s, span, :] for s in into]
        for n in range(ITEMS):
            if n < PEERS:
                line = tag_recv[n, pl.ds(c, 1), :]
            else:
                way, i = (n - PEERS) // 2, (n - PEERS) % 2
                line = tag_recv[PEERS + way, pl.ds(2 * c + i, 1), :]
            tag = jnp.broadcast_to(line, (rows, width))
            item = recv[t, part, n]
            totals = [x - jnp.where(tag == j, item, 0.0) for x, j in zip(totals, targets)]
        for s, x in zip(into, totals):
            resid[s, span, :] = x

    def solve(t, part, first):
        c = t % COLORS
        span = pl.ds(part * rows, rows)
        if not first:
            all_copies(t - 1, part).wait_recv()
            gather(t - 1, part, pair(c))
        changes = []
        for s in pair(c):
            new = jnp.dot(
                resid[s, span, :].astype(jnp.bfloat16), diag[jrow[s]], preferred_element_type=jnp.float32
            )
            changes.append((new - solb[s, span, :]).astype(jnp.bfloat16))
            solb[s, span, :] = new
        owners = [jrow[s] for s in pair(c)]
        if first and part == 0:
            loads[5].wait()
            loads[6].wait()
            loads[7].wait()

        def products(i, k):
            both = jnp.concatenate([coup[owners[i], k], coup[owners[i], k + 1]], axis=1)
            out = jnp.dot(changes[i], both, preferred_element_type=jnp.float32)
            return out[:, :width], out[:, width:]

        terms = [products(i, 2) for i in range(2)]
        wants = [[jnp.full((rows, width), gpeer[k, j], jnp.int32) for k in range(2)] for j in owners]
        if first and part == 0:
            pl.semaphore_wait(barrier, ENDS)
        for n, q in enumerate(peers):
            sums = [
                jnp.where(want[0] == q, term[0], jnp.where(want[1] == q, term[1], 0.0))
                for want, term in zip(wants, terms)
            ]
            send[t % 2, part, n] = sums[0] + sums[1]
            copy(t, part, n).start()
        for i in range(2):
            send[t % 2, part, PEERS + i], send[t % 2, part, PEERS + 2 + i] = products(i, 4)
        for n in range(PEERS, ENDS):
            copy(t, part, n).start()
        for i in range(2):
            near[part, i, 0], near[part, i, 1] = products(i, 0)

    def local(t, part):
        c = t % COLORS
        span = pl.ds(part * rows, rows)
        into = pair(c + 1) + pair(c + 2) + pair(c + 3)
        targets = [jrow[s] for s in into]
        totals = [resid[s, span, :] for s in into]
        for i, s in enumerate(pair(c)):
            for k in range(2):
                tag = jnp.full((rows, width), ltgt[k, jrow[s]], jnp.int32)
                item = near[part, i, k]
                totals = [x - jnp.where(tag == j, item, 0.0) for x, j in zip(totals, targets)]
        for s, x in zip(into, totals):
            resid[s, span, :] = x

    loads[3].wait()
    for s, j in enumerate(slots):
        resid[s] = rhs[j]
    loads[4].wait()
    solve(0, 0, True)

    loads[1].wait()
    loads[2].wait()
    line = lax.broadcasted_iota(jnp.int32, (8, width), 0)
    for n, q in enumerate(peers):
        tile = jnp.full((8, width), -1, jnp.int32)
        for c in range(COLORS):
            tile = jnp.where(line == c, glist[0, c, q], tile)
        tag_send[n] = tile
        tag_copy(n).start()
    for way in range(2):
        tile = jnp.full((8, width), -1, jnp.int32)
        for s, j in enumerate(slots):
            tile = jnp.where(line == s, dtgt[way, j], tile)
        tag_send[PEERS + way] = tile
        tag_copy(PEERS + way).start()

    for part in range(1, parts):
        solve(0, part, True)
    for part in range(parts):
        local(0, part)
    all_tags().wait_recv()

    def step(t, carry):
        for part in range(parts):
            @pl.when(t >= 2)
            def _():
                all_copies(t, part).wait_send()

            solve(t, part, False)
            local(t, part)
            gather(t - 1, part, pair(t + 1) + pair(t + 2))
        return carry

    lax.fori_loop(1, STEPS, step, 0)
    for r in range(rows_dev):
        sol_out[r] = solb[rank[r]]
    last = STEPS - 1
    for part in range(parts):
        all_copies(last, part).wait_recv()
        gather(last, part, pair(0) + pair(1) + pair(2))
    for r in range(rows_dev):
        def_out[r] = resid[rank[r]]
    for part in range(parts):
        all_copies(last - 1, part).wait_send()
        all_copies(last, part).wait_send()
    all_tags().wait_send()


def on_device(coupling, diag_inv, rhs, color, local_target, group_peer, group_list, dom_target):
    rows_dev, rhs_count, width = rhs.shape
    parts, rows = STREAMS, rhs_count // STREAMS
    anywhere, vmem = pl.BlockSpec(memory_space=pl.ANY), pl.BlockSpec(memory_space=pltpu.VMEM)
    ints = [color, local_target.T, group_peer.T, group_list, dom_target.T]
    return pl.pallas_call(
        functools.partial(kernel, parts, lax.axis_size("dom")),
        out_shape=(pltpu.VMEM(rhs.shape, jnp.float32), pltpu.VMEM(rhs.shape, jnp.float32)),
        in_specs=[anywhere] * 8,
        out_specs=(vmem, vmem),
        scratch_shapes=[
            pltpu.VMEM(coupling.shape, coupling.dtype),
            pltpu.VMEM(diag_inv.shape, diag_inv.dtype),
            pltpu.VMEM(rhs.shape, rhs.dtype),
            *[pltpu.SMEM(x.shape, x.dtype) for x in ints],
            pltpu.VMEM((STEPS, parts, ITEMS, rows, width), jnp.float32),
            pltpu.VMEM((2, parts, ITEMS, rows, width), jnp.float32),
            pltpu.VMEM((ENDS, 8, width), jnp.int32),
            pltpu.VMEM((ENDS, 8, width), jnp.int32),
            pltpu.VMEM((rows_dev, rhs_count, width), jnp.float32),
            pltpu.VMEM((rows_dev, rhs_count, width), jnp.float32),
            pltpu.VMEM((parts, 2, 2, rows, width), jnp.float32),
            pltpu.SMEM((rows_dev,), jnp.int32),
            pltpu.SMEM((rows_dev,), jnp.int32),
            pltpu.SemaphoreType.DMA((8,)),
            pltpu.SemaphoreType.DMA((2, parts)),
            pltpu.SemaphoreType.DMA((2, parts)),
            pltpu.SemaphoreType.DMA,
            pltpu.SemaphoreType.DMA,
        ],
        compiler_params=pltpu.CompilerParams(collective_id=0, has_side_effects=True),
        name="sweeps",
    )(coupling, diag_inv, rhs, *ints)


def solution(mesh):
    placed = (
        P(("dom", "sub"), None, None, None),
        P(("dom", "sub"), None, None),
        P(("dom", "sub"), None, None),
        P(("dom", "sub")),
        P(("dom", "sub"), None),
        P(("dom", "sub"), None),
        P(("dom", "sub"), None, None),
        P(("dom", "sub"), None),
    )
    return jax.shard_map(
        on_device,
        mesh=mesh,
        in_specs=placed,
        out_specs=(P(("dom", "sub"), None, None), P(("dom", "sub"), None, None)),
        check_vma=False,
    )
```

time: 82.2 us -> 69.2 us (0.84)
  Pallas kernels: 73.6 us -> 66.6 us
  local copies, waits for them, and re-layouts: 7.37 us -> 1.41 us
    pallas_call x1, Pallas kernels: 73.6 us -> 66.6 us  [on_device(): pl.pallas_call(functools.partial(kernel, parts, lax.axis_size('dom')), ou...]
    unnamed x5 -> x2, local copies, waits for them, and re-layouts: 7.37 us -> 1.41 us
where the time goes in v2:
time: 69.2 us; the launch traced here: 68.7 us
  Pallas kernels  66.6 us (96%)
  local copies, waits for them, and re-layouts  1.41 us (2%)
    pallas_call x1, Pallas kernels, on_device(): pl.pallas_call(functools.partial(kernel, parts, lax.axis_size('dom')), ou...  66.6 us
    unnamed x2, local copies, waits for them, and re-layouts  1.41 us

profile of v2, /device:TPU:6, one launch (start us, length us, event | category | flops | bytes accessed | tf_op | source)
XLA Modules:
  0.0 68.7 jit_solution(1428683859432371685)
XLA Ops:
  0.6 66.6 %sweeps.1 = (f32[8,64,128]{2,1,0:T(8,128)S(1)}, f32[8,64,128]{2,1,0:T(8,128)S(1)}) custom-call(bf16[8,6,128,128]{3,2,1,0:T(8,128)(2,1)} %coup_in.1, bf16[8,128,128]{2,1,0:T(8,128)(2,1)} %diag_in.1, f32[8,64,128]{2,1,0:T(8,128)} %rhs_in.1, s32[8]{0:T(128)} %color_in.1, s32[2,8]{1,0:T(2,128)} %bitcast.3, s32[2,8]{1,0:T(2,128)} %bitcast.4, ...), custom_call_target="tpu_custom_call" | custom-call | tf_op jit(solution)/shard_map/sweeps/pallas_call | solution.py:230
  67.3 0.7 %copy.12 = f32[8,64,128]{2,1,0:T(8,128)} copy(f32[8,64,128]{2,1,0:T(8,128)S(1)} %get-tuple-element.2) | data formatting | bytes 524288
  68.0 0.7 %copy.13 = f32[8,64,128]{2,1,0:T(8,128)} copy(f32[8,64,128]{2,1,0:T(8,128)S(1)} %get-tuple-element.3) | data formatting | bytes 524288

commit v3 on v2

--- a/solution.py
+++ b/solution.py
@@ -14,7 +14,7 @@
 SIDE = 4
 OFFSETS = sorted(
     [(dx, dy) for dy in range(SIDE) for dx in range(SIDE) if (dx, dy) != (0, 0)],
-    key=lambda o: -(min(o[0], SIDE - o[0]) + min(o[1], SIDE - o[1])),
+    key=lambda o: (-min(o[0], SIDE - o[0]) * (3 if min(o[1], SIDE - o[1]) else 2) - 2 * min(o[1], SIDE - o[1])),
 )
 PEERS = len(OFFSETS)
 ENDS = PEERS + 2
@@ -138,19 +138,19 @@
 
         terms = [products(i, 2) for i in range(2)]
         wants = [[jnp.full((rows, width), gpeer[k, j], jnp.int32) for k in range(2)] for j in owners]
-        if first and part == 0:
-            pl.semaphore_wait(barrier, ENDS)
         for n, q in enumerate(peers):
             sums = [
                 jnp.where(want[0] == q, term[0], jnp.where(want[1] == q, term[1], 0.0))
                 for want, term in zip(wants, terms)
             ]
             send[t % 2, part, n] = sums[0] + sums[1]
-            copy(t, part, n).start()
+            if not first:
+                copy(t, part, n).start()
         for i in range(2):
             send[t % 2, part, PEERS + i], send[t % 2, part, PEERS + 2 + i] = products(i, 4)
-        for n in range(PEERS, ENDS):
-            copy(t, part, n).start()
+        if not first:
+            for n in range(PEERS, ENDS):
+                copy(t, part, n).start()
         for i in range(2):
             near[part, i, 0], near[part, i, 1] = products(i, 0)
 
@@ -172,7 +172,8 @@
     for s, j in enumerate(slots):
         resid[s] = rhs[j]
     loads[4].wait()
-    solve(0, 0, True)
+    for part in range(parts):
+        solve(0, part, True)
 
     loads[1].wait()
     loads[2].wait()
@@ -182,16 +183,19 @@
         for c in range(COLORS):
             tile = jnp.where(line == c, glist[0, c, q], tile)
         tag_send[n] = tile
-        tag_copy(n).start()
     for way in range(2):
         tile = jnp.full((8, width), -1, jnp.int32)
         for s, j in enumerate(slots):
             tile = jnp.where(line == s, dtgt[way, j], tile)
         tag_send[PEERS + way] = tile
-        tag_copy(PEERS + way).start()
-
-    for part in range(1, parts):
-        solve(0, part, True)
+
+    pl.semaphore_wait(barrier, ENDS)
+    for part in range(parts):
+        for n in range(ENDS):
+            copy(0, part, n).start()
+        if part == 0:
+            for n in range(ENDS):
+                tag_copy(n).start()
     for part in range(parts):
         local(0, part)
     all_tags().wait_recv()

time: 69.2 us -> 69.1 us (level)
  no operation moved by 1% of the time
where the time goes in v3:
time: 69.1 us; the launch traced here: 68.4 us
  Pallas kernels  66.3 us (96%)
  local copies, waits for them, and re-layouts  1.41 us (2%)
    pallas_call x1, Pallas kernels, on_device(): pl.pallas_call(functools.partial(kernel, parts, lax.axis_size('dom')), ou...  66.3 us
    unnamed x2, local copies, waits for them, and re-layouts  1.41 us

profile of v3, /device:TPU:6, one launch (start us, length us, event | category | flops | bytes accessed | tf_op | source)
XLA Modules:
  0.0 68.4 jit_solution(3170184895874013554)
XLA Ops:
  0.6 66.3 %sweeps.1 = (f32[8,64,128]{2,1,0:T(8,128)S(1)}, f32[8,64,128]{2,1,0:T(8,128)S(1)}) custom-call(bf16[8,6,128,128]{3,2,1,0:T(8,128)(2,1)} %coup_in.1, bf16[8,128,128]{2,1,0:T(8,128)(2,1)} %diag_in.1, f32[8,64,128]{2,1,0:T(8,128)} %rhs_in.1, s32[8]{0:T(128)} %color_in.1, s32[2,8]{1,0:T(2,128)} %bitcast.3, s32[2,8]{1,0:T(2,128)} %bitcast.4, ...), custom_call_target="tpu_custom_call" | custom-call | tf_op jit(solution)/shard_map/sweeps/pallas_call | solution.py:234
  67.0 0.7 %copy.12 = f32[8,64,128]{2,1,0:T(8,128)} copy(f32[8,64,128]{2,1,0:T(8,128)S(1)} %get-tuple-element.2) | data formatting | bytes 524288
  67.7 0.7 %copy.13 = f32[8,64,128]{2,1,0:T(8,128)} copy(f32[8,64,128]{2,1,0:T(8,128)S(1)} %get-tuple-element.3) | data formatting | bytes 524288
